TPU v7x, 256 devices: a whole 4x4x8 slice. The times are simulated.
256 devices in a mesh: dp: 2 (over x_hi), mx: 8 (over z), my: 16 (over x_lo, y, core).
Axes of the slice: x: 4 (x_hi: 2, x_lo: 2; x = x_hi * 2 + x_lo), y: 4, z: 8, core: 2. Of those that a mesh axis runs over, the one named last changes fastest.
Arguments:
- inputs: bfloat16 [2048, 6144], P(('dp', 'my'), 'mx'), may hold values from -6 to 6
- hidden_in: bfloat16 [2048, 24576], P(('dp', 'mx'), 'my'), may hold values from -6 to 6
- out_grad: bfloat16 [2048, 6144], P(('dp', 'my'), 'mx'), may hold values from -6 to 6
- up_weight: bfloat16 [6144, 24576], P('mx', 'my'), may hold values from -0.078125 to 0.078125
- down_weight: bfloat16 [24576, 6144], P('my', 'mx'), may hold values from -0.0390625 to 0.0390625
Outputs:
- inputs_grad: bfloat16 [2048, 6144], P(('dp', 'my'), 'mx')
- up_grad: bfloat16 [6144, 24576], P('mx', 'my')
- down_grad: bfloat16 [24576, 6144], P('my', 'mx')
All inputs are finite; a program needn't handle non-finite values.
Results may differ from a plain program's by a relative error of at most 0.0059.
Values may be sent and summed in bfloat16 or wider, within the bound.
No kernel may reach another device: no remote copies, remote signals or barrier semaphores. Data moves between devices by JAX's collectives and lax.ppermute only.
A program may use at most 64 MiB of HBM per device.

v0:
```python
import jax
import jax.numpy as jnp
from jax import lax
from jax.sharding import PartitionSpec as P


def gelu_value(value):
    return 0.5 * value * (1.0 + lax.erf(value * 0.7071067811865476))


def gelu_slope(value):
    return (
        0.5 * (1.0 + lax.erf(value * 0.7071067811865476))
        + value * jnp.exp(-0.5 * value * value) * 0.3989422804014327
    )


def per_device(inputs, hidden_in, out_grad, up_weight, down_weight):
    total_tokens = out_grad.shape[0] * lax.axis_size("my") * lax.axis_size("dp")
    grad_scale = 1.0 / jnp.sqrt(jnp.float32(total_tokens))
    pre_value = hidden_in.astype(jnp.float32)
    act_local = gelu_value(pre_value).astype(jnp.bfloat16)
    act_whole = lax.all_gather(act_local, "mx", axis=0, tiled=True)
    input_whole, grad_whole = (
        lax.all_gather(inputs, "my", axis=0, tiled=True),
        lax.all_gather(out_grad, "my", axis=0, tiled=True),
    )
    down_part = (
        jnp.einsum("tf,td->fd", act_whole, grad_whole, preferred_element_type=jnp.float32)
        * grad_scale
    )
    row_block = grad_whole
    act_grad = lax.psum_scatter(
        jnp.einsum("td,fd->tf", row_block, down_weight, preferred_element_type=jnp.float32),
        "mx",
        scatter_dimension=0,
        tiled=True,
    )
    pre_grad = (act_grad * gelu_slope(pre_value)).astype(jnp.bfloat16)
    pre_whole = lax.all_gather(pre_grad, "mx", axis=0, tiled=True)
    row_block = pre_whole
    inputs_grad = lax.psum_scatter(
        jnp.einsum("tf,df->td", row_block, up_weight, preferred_element_type=jnp.float32),
        "my",
        scatter_dimension=0,
        tiled=True,
    ).astype(jnp.bfloat16)
    up_part = (
        jnp.einsum("td,tf->df", input_whole, pre_whole, preferred_element_type=jnp.float32)
        * grad_scale
    )
    up_total, down_total = (
        lax.psum(up_part.astype(jnp.bfloat16), "dp").astype(jnp.float32),
        lax.psum(down_part.astype(jnp.bfloat16), "dp").astype(jnp.float32),
    )
    return (inputs_grad, up_total.astype(jnp.bfloat16), down_total.astype(jnp.bfloat16))


def solution(mesh):
    return jax.shard_map(
        per_device,
        mesh=mesh,
        in_specs=(
            P(("dp", "my"), "mx"),
            P(("dp", "mx"), "my"),
            P(("dp", "my"), "mx"),
            P("mx", "my"),
            P("my", "mx"),
        ),
        out_specs=(P(("dp", "my"), "mx"), P("mx", "my"), P("my", "mx")),
        check_vma=False,
    )
```

profile of v0, /device:TPU:4, one launch (start us, length us, event | category | flops | bytes accessed | tf_op | source)
XLA Modules:
  0.0 477.7 jit_solution(6515074767499462279)
XLA Ops:
  7.2 0.7 all-gather.5.cloned.1.call-update
  7.9 0.0 reduce-scatter.3.cloned.1.call-start
  8.0 40.1 %all-gather.5.cloned.1.call-done = bf16[1024,768]{1,0:T(8,128)(2,1)} async-done(((bf16[64,768]{1,0:T(8,128)(2,1)}), bf16[1024,768]{1,0:T(8,128)(2,1)}) %all-gather.5.cloned.1.call-update) | async-done | bytes 1572880 | tf_op jit(solution)/shard_map/all_gather | solution.py:26
  48.1 6.0 %fusion.10 = f32[1024,1536]{1,0:T(8,128)} fusion(bf16[1024,768]{1,0:T(8,128)(2,1)} %all-gather.5.cloned.1.call-done, bf16[1536,768]{1,0:T(8,128)(2,1)S(1)} %copy-done), kind=kOutput, calls=%fused_computation.17 | convolution fusion | flops 2415919104 | bytes 10223616 | tf_op jit(solution)/shard_map/td,fd->tf/dot_general | solution.py:34
  54.1 0.0 all-gather.11.cloned.1.call-start
  54.1 75.5 %reduce-scatter.3.cloned.1.call-done = f32[128,1536]{1,0:T(8,128)} async-done(((f32[1024,1536]{1,0:T(8,128)}), f32[128,1536]{1,0:T(8,128)}) %reduce-scatter.3.cloned.1.call-update) | async-done | bytes 786448 | tf_op jit(solution)/shard_map/reduce_scatter | solution.py:33
  129.6 2.4 fusion.9
  132.0 0.0 all-gather.9.cloned.1.call-start
  132.1 0.5 all-gather.9.cloned.1.call-update
  132.6 0.0 all-gather.7.cloned.1.call-start
  132.7 0.5 all-gather.7.cloned.1.call-update
  133.2 0.0 all-reduce.3.cloned.1.call-start
  133.3 42.5 %all-gather.11.cloned.1.call-done = bf16[1024,1536]{1,0:T(8,128)(2,1)} async-done(((bf16[128,1536]{1,0:T(8,128)(2,1)}), bf16[1024,1536]{1,0:T(8,128)(2,1)}) %all-gather.11.cloned.1.call-update) | async-done | bytes 3145744 | tf_op jit(solution)/shard_map/all_gather | solution.py:23
  175.8 6.4 %multiply_convert_fusion = bf16[1536,768]{1,0:T(8,128)(2,1)} fusion(bf16[1024,1536]{1,0:T(8,128)(2,1)} %all-gather.11.cloned.1.call-done, bf16[1024,768]{1,0:T(8,128)(2,1)} %all-gather.5.cloned.1.call-done), kind=kOutput, calls=%fused_computation | convolution fusion | flops 2418278400 | bytes 7077888 | tf_op jit(solution)/shard_map/tf,td->fd/dot_general | solution.py:29
  182.2 29.2 %all-gather.9.cloned.1.call-done = bf16[1024,768]{1,0:T(8,128)(2,1)} async-done(((bf16[64,768]{1,0:T(8,128)(2,1)}), bf16[1024,768]{1,0:T(8,128)(2,1)}) %all-gather.9.cloned.1.call-update) | async-done | bytes 1572880 | tf_op jit(solution)/shard_map/all_gather | solution.py:25
  211.4 46.9 %all-gather.7.cloned.1.call-done = bf16[1024,1536]{1,0:T(8,128)(2,1)} async-done(((bf16[128,1536]{1,0:T(8,128)(2,1)}), bf16[1024,1536]{1,0:T(8,128)(2,1)}) %all-gather.7.cloned.1.call-update) | async-done | bytes 3145744 | tf_op jit(solution)/shard_map/all_gather | solution.py:40
  258.3 6.4 %fusion = bf16[768,1536]{0,1:T(8,128)(2,1)} fusion(bf16[1024,1536]{1,0:T(8,128)(2,1)} %all-gather.7.cloned.1.call-done, bf16[1024,768]{1,0:T(8,128)(2,1)} %all-gather.9.cloned.1.call-done), kind=kOutput, calls=%fused_computation.2 | convolution fusion | flops 2418278400 | bytes 7077888 | tf_op jit(solution)/shard_map/td,tf->df/dot_general | solution.py:49
  264.8 0.0 reduce-scatter.5.cloned.1.call-start
  264.8 6.9 %fusion.11 = f32[1024,768]{1,0:T(8,128)} fusion(bf16[1024,1536]{1,0:T(8,128)(2,1)} %all-gather.7.cloned.1.call-done, bf16[768,1536]{1,0:T(8,128)(2,1)} %param.8), kind=kOutput, calls=%fused_computation.18 | convolution fusion | flops 2415919104 | bytes 8650752 | tf_op jit(solution)/shard_map/tf,df->td/dot_general | solution.py:43
  271.8 121.6 %all-reduce.3.cloned.1.call-done = (bf16[768,1536]{0,1:T(8,128)(2,1)}, bf16[1536,768]{1,0:T(8,128)(2,1)}) async-done(((bf16[768,1536]{0,1:T(8,128)(2,1)}, bf16[1536,768]{1,0:T(8,128)(2,1)}), (bf16[768,1536]{0,1:T(8,128)(2,1)}, bf16[1536,768]{1,0:T(8,128)(2,1)})) %all-reduce.3.cloned.1.call-update) | async-done | bytes 4718608 | tf_op jit(solution)/shard_map/psum | solution.py:53
  393.4 4.3 copy.8
  397.7 68.3 %reduce-scatter.5.cloned.1.call-done = f32[64,768]{1,0:T(8,128)} async-done(((f32[1024,768]{1,0:T(8,128)}), f32[64,768]{1,0:T(8,128)}) %reduce-scatter.5.cloned.1.call-update) | async-done | bytes 196624 | tf_op jit(solution)/shard_map/reduce_scatter | solution.py:42
  466.0 1.6 convert_element_type.27
  467.6 3.2 copy.11
  (9 shorter events, 0.1 us)
Async XLA Ops:
  7.2 40.9 %copy-start = (bf16[1536,768]{1,0:T(8,128)(2,1)S(1)}, bf16[1536,768]{1,0:T(8,128)(2,1)}, u32[]{:S(2)}) copy-start(bf16[1536,768]{1,0:T(8,128)(2,1)} %param.9) | copy-start | bytes 7077892
  7.2 40.9 %all-gather.5.cloned.1.call-start = ((), (), s32[]{:S(2)}) async-start(), calls=%async_computation.2 | async-start | bytes 1671168 | tf_op jit(solution)/shard_map/all_gather | solution.py:26
  7.9 121.7 %reduce-scatter.3.cloned.1.call-start = ((), (), s32[]{:S(2)}) async-start(), calls=%async_computation.3 | async-start | bytes 7077888 | tf_op jit(solution)/shard_map/reduce_scatter | solution.py:33
  54.0 75.6 %copy-start.1 = (bf16[128,1536]{1,0:T(8,128)(2,1)S(1)}, bf16[128,1536]{1,0:T(8,128)(2,1)}, u32[]{:S(2)}) copy-start(bf16[128,1536]{1,0:T(8,128)(2,1)} %param.6) | copy-start | bytes 1179652
  54.1 121.8 %all-gather.11.cloned.1.call-start = ((), (), s32[]{:S(2)}) async-start(), calls=%async_computation.7 | async-start | bytes 3538944 | tf_op jit(solution)/shard_map/all_gather | solution.py:23
  132.0 79.4 %all-gather.9.cloned.1.call-start = ((), (), s32[]{:S(2)}) async-start(), calls=%async_computation.6 | async-start | bytes 1671168 | tf_op jit(solution)/shard_map/all_gather | solution.py:25
  132.6 125.7 %all-gather.7.cloned.1.call-start = ((), (), s32[]{:S(2)}) async-start(), calls=%async_computation.4 | async-start | bytes 3538944 | tf_op jit(solution)/shard_map/all_gather | solution.py:40
  133.2 260.2 %all-reduce.3.cloned.1.call-start = ((), (), s32[]{:S(2)}) async-start(), calls=%async_computation.8 | async-start | bytes 9437184 | tf_op jit(solution)/shard_map/psum | solution.py:53
  264.8 201.2 %reduce-scatter.5.cloned.1.call-start = ((), (), s32[]{:S(2)}) async-start(), calls=%async_computation.5 | async-start | bytes 3342336 | tf_op jit(solution)/shard_map/reduce_scatter | solution.py:42
Sparse Core Ops, SparseCore 0:
  9.8 38.1 all-gather.4
  54.2 75.3 reduce-scatter.2
  132.2 43.5 all-gather.10
  177.5 33.8 all-gather.8
  213.1 45.2 all-gather.6
  264.9 128.4 all-reduce.2
  396.0 70.0 reduce-scatter.4
where the time goes:
time: 478 us
  waiting for transfers between devices  426 us (89%)
  matrix products  25.8 us (5%)
  between operations  14.1 us (3%)
  local copies, waits for them, and re-layouts  7.51 us (2%)
    psum x1, waiting for transfers between devices, per_device(): lax.psum(up_part.astype(jnp.bfloat16), 'dp').astype(jnp.float32)  122 us
    reduce_scatter x1, waiting for transfers between devices, per_device(): lax.psum_scatter(jnp.einsum('td,fd->tf', row_block, down_weight, preferre...  75.5 us
    reduce_scatter x1, waiting for transfers between devices, per_device(): lax.psum_scatter(jnp.einsum('tf,df->td', row_block, up_weight, preferred_...  68.3 us
    all_gather x1, waiting for transfers between devices, per_device(): pre_whole = lax.all_gather(pre_grad, 'mx', axis=0, tiled=True)  46.9 us
    all_gather x1, waiting for transfers between devices, per_device(): act_whole = lax.all_gather(act_local, 'mx', axis=0, tiled=True)  42.5 us
    all_gather x1, waiting for transfers between devices, per_device(): lax.all_gather(out_grad, 'my', axis=0, tiled=True)  40.1 us
    all_gather x1, waiting for transfers between devices, per_device(): lax.all_gather(inputs, 'my', axis=0, tiled=True)  29.2 us
  transfers between devices with their start and end apart: 7, of which 7 were waited for; matrix products, arithmetic and copies ran while one was open for 4% of the time, Pallas kernels for 0%

commit v1 on v0

--- a/solution.py
+++ b/solution.py
@@ -2,6 +2,11 @@
 import jax.numpy as jnp
 from jax import lax
 from jax.sharding import PartitionSpec as P
+
+
+def all_by_exchange(block, axis, along):
+    sent = jnp.stack([block] * lax.axis_size(axis))
+    return jnp.concatenate(lax.all_to_all(sent, axis, 0, 0), axis=along)
 
 
 def gelu_value(value):
@@ -22,7 +27,7 @@
     act_local = gelu_value(pre_value).astype(jnp.bfloat16)
     act_whole = lax.all_gather(act_local, "mx", axis=0, tiled=True)
     input_whole, grad_whole = (
-        lax.all_gather(inputs, "my", axis=0, tiled=True),
+        all_by_exchange(inputs, "my", 0),
         lax.all_gather(out_grad, "my", axis=0, tiled=True),
     )
     down_part = (

time: 478 us -> 441 us (0.923)
  waiting for transfers between devices: 426 us -> 382 us
  starting transfers between devices: 0.28 us -> 5.29 us
    all_gather x1 -> x0, waiting for transfers between devices: 29.2 us -> none  [per_device(): lax.all_gather(inputs, 'my', axis=0, tiled=True)]
    all_gather x1, waiting for transfers between devices: 46.9 us -> 38.9 us  [per_device(): pre_whole = lax.all_gather(pre_grad, 'mx', axis=0, tiled=True)]
    all_gather x1, waiting for transfers between devices: 42.5 us -> 36.8 us  [per_device(): act_whole = lax.all_gather(act_local, 'mx', axis=0, tiled=True)]
    all_to_all x0 -> x1, starting transfers between devices: none -> 5.05 us  [all_by_exchange(): return jnp.concatenate(lax.all_to_all(sent, axis, 0, 0), axis=along)]
  transfers between devices with their start and end apart: 7 -> 7, of which waited for: 7 -> 6; matrix products, arithmetic and copies ran while one was open for 4% -> 4% of each run, Pallas kernels for 0% -> 0%
where the time goes in v1:
time: 441 us; the launch traced here: 440 us
  waiting for transfers between devices  382 us (87%)
  matrix products  25.8 us (6%)
  between operations  14.1 us (3%)
  local copies, waits for them, and re-layouts  8.82 us (2%)
  starting transfers between devices  5.29 us (1%)
    psum x1, waiting for transfers between devices, per_device(): lax.psum(up_part.astype(jnp.bfloat16), 'dp').astype(jnp.float32)  122 us
    reduce_scatter x1, waiting for transfers between devices, per_device(): lax.psum_scatter(jnp.einsum('td,fd->tf', row_block, down_weight, preferre...  75.5 us
    reduce_scatter x1, waiting for transfers between devices, per_device(): lax.psum_scatter(jnp.einsum('tf,df->td', row_block, up_weight, preferred_...  68.2 us
    all_gather x1, waiting for transfers between devices, per_device(): lax.all_gather(out_grad, 'my', axis=0, tiled=True)  40.1 us
    all_gather x1, waiting for transfers between devices, per_device(): pre_whole = lax.all_gather(pre_grad, 'mx', axis=0, tiled=True)  38.9 us
    all_gather x1, waiting for transfers between devices, per_device(): act_whole = lax.all_gather(act_local, 'mx', axis=0, tiled=True)  36.8 us
  transfers between devices with their start and end apart: 7, of which 6 were waited for; matrix products, arithmetic and copies ran while one was open for 4% of the time, Pallas kernels for 0%

profile of v1, /device:TPU:4, one launch (start us, length us, event | category | flops | bytes accessed | tf_op | source)
XLA Modules:
  0.0 440.3 jit_solution(10240796397283746341)
XLA Ops:
  7.2 0.0 all-gather.4.cloned.1.call-start
  7.2 0.7 all-gather.4.cloned.1.call-update
  7.9 0.0 reduce-scatter.3.cloned.1.call-start
  8.0 40.1 %all-gather.4.cloned.1.call-done = bf16[1024,768]{1,0:T(8,128)(2,1)} async-done(((bf16[64,768]{1,0:T(8,128)(2,1)}), bf16[1024,768]{1,0:T(8,128)(2,1)}) %all-gather.4.cloned.1.call-update) | async-done | bytes 1572880 | tf_op jit(solution)/shard_map/all_gather | solution.py:31
  48.1 6.0 %fusion.10 = f32[1024,1536]{1,0:T(8,128)} fusion(bf16[1024,768]{1,0:T(8,128)(2,1)} %all-gather.4.cloned.1.call-done, bf16[1536,768]{1,0:T(8,128)(2,1)S(1)} %copy-done), kind=kOutput, calls=%fused_computation.17 | convolution fusion | flops 2415919104 | bytes 10223616 | tf_op jit(solution)/shard_map/td,fd->tf/dot_general | solution.py:39
  54.1 0.0 all-gather.8.cloned.1.call-start
  54.1 75.5 %reduce-scatter.3.cloned.1.call-done = f32[128,1536]{1,0:T(8,128)} async-done(((f32[1024,1536]{1,0:T(8,128)}), f32[128,1536]{1,0:T(8,128)}) %reduce-scatter.3.cloned.1.call-update) | async-done | bytes 786448 | tf_op jit(solution)/shard_map/reduce_scatter | solution.py:38
  129.6 2.4 fusion.9
  132.0 0.0 all-gather.6.cloned.1.call-start
  132.1 0.5 all-gather.6.cloned.1.call-update
  132.6 1.3 stack.2
  133.9 5.0 %all-to-all-start = ((bf16[16,64,768]{2,1,0:T(8,128)(2,1)}), bf16[16,64,768]{2,1,0:T(8,128)(2,1)}, u32[]{:S(2)}, u32[]{:S(2)}) async-start(bf16[16,64,768]{2,1,0:T(8,128)(2,1)} %stack.2), calls=%async_computation.2 | async-start | bytes 3145728 | tf_op jit(solution)/shard_map/all_to_all | solution.py:9
  139.0 0.0 all-reduce.3.cloned.1.call-start
  139.0 36.8 %all-gather.8.cloned.1.call-done = bf16[1024,1536]{1,0:T(8,128)(2,1)} async-done(((bf16[128,1536]{1,0:T(8,128)(2,1)}), bf16[1024,1536]{1,0:T(8,128)(2,1)}) %all-gather.8.cloned.1.call-update) | async-done | bytes 3145744 | tf_op jit(solution)/shard_map/all_gather | solution.py:28
  175.8 6.4 %multiply_convert_fusion = bf16[1536,768]{1,0:T(8,128)(2,1)} fusion(bf16[1024,1536]{1,0:T(8,128)(2,1)} %all-gather.8.cloned.1.call-done, bf16[1024,768]{1,0:T(8,128)(2,1)} %all-gather.4.cloned.1.call-done), kind=kOutput, calls=%fused_computation | convolution fusion | flops 2418278400 | bytes 7077888 | tf_op jit(solution)/shard_map/tf,td->fd/dot_general | solution.py:34
  182.2 38.9 %all-gather.6.cloned.1.call-done = bf16[1024,1536]{1,0:T(8,128)(2,1)} async-done(((bf16[128,1536]{1,0:T(8,128)(2,1)}), bf16[1024,1536]{1,0:T(8,128)(2,1)}) %all-gather.6.cloned.1.call-update) | async-done | bytes 3145744 | tf_op jit(solution)/shard_map/all_gather | solution.py:45
  221.1 6.4 %fusion = bf16[768,1536]{0,1:T(8,128)(2,1)} fusion(bf16[1024,1536]{1,0:T(8,128)(2,1)} %all-gather.6.cloned.1.call-done, bf16[1024,768]{1,0:T(8,128)(2,1)} %bitcast), kind=kOutput, calls=%fused_computation.2 | convolution fusion | flops 2418278400 | bytes 7077888 | tf_op jit(solution)/shard_map/td,tf->df/dot_general | solution.py:54
  227.6 0.0 reduce-scatter.5.cloned.1.call-start
  227.6 6.9 %fusion.11 = f32[1024,768]{1,0:T(8,128)} fusion(bf16[1024,1536]{1,0:T(8,128)(2,1)} %all-gather.6.cloned.1.call-done, bf16[768,1536]{1,0:T(8,128)(2,1)} %param.8), kind=kOutput, calls=%fused_computation.18 | convolution fusion | flops 2415919104 | bytes 8650752 | tf_op jit(solution)/shard_map/tf,df->td/dot_general | solution.py:48
  234.6 121.6 %all-reduce.3.cloned.1.call-done = (bf16[768,1536]{0,1:T(8,128)(2,1)}, bf16[1536,768]{1,0:T(8,128)(2,1)}) async-done(((bf16[768,1536]{0,1:T(8,128)(2,1)}, bf16[1536,768]{1,0:T(8,128)(2,1)}), (bf16[768,1536]{0,1:T(8,128)(2,1)}, bf16[1536,768]{1,0:T(8,128)(2,1)})) %all-reduce.3.cloned.1.call-update) | async-done | bytes 4718608 | tf_op jit(solution)/shard_map/psum | solution.py:58
  356.2 4.3 copy.8
  360.5 68.2 %reduce-scatter.5.cloned.1.call-done = f32[64,768]{1,0:T(8,128)} async-done(((f32[1024,768]{1,0:T(8,128)}), f32[64,768]{1,0:T(8,128)}) %reduce-scatter.5.cloned.1.call-update) | async-done | bytes 196624 | tf_op jit(solution)/shard_map/reduce_scatter | solution.py:47
  428.7 1.6 convert_element_type.27
  430.2 3.2 copy.11
  (11 shorter events, 0.1 us)
Async XLA Ops:
  7.2 40.9 %copy-start = (bf16[1536,768]{1,0:T(8,128)(2,1)S(1)}, bf16[1536,768]{1,0:T(8,128)(2,1)}, u32[]{:S(2)}) copy-start(bf16[1536,768]{1,0:T(8,128)(2,1)} %param.9) | copy-start | bytes 7077892
  7.2 40.9 %all-gather.4.cloned.1.call-start = ((), (), s32[]{:S(2)}) async-start(), calls=%async_computation.3 | async-start | bytes 1671168 | tf_op jit(solution)/shard_map/all_gather | solution.py:31
  7.9 121.7 %reduce-scatter.3.cloned.1.call-start = ((), (), s32[]{:S(2)}) async-start(), calls=%async_computation.4 | async-start | bytes 7077888 | tf_op jit(solution)/shard_map/reduce_scatter | solution.py:38
  54.0 75.6 %copy-start.1 = (bf16[128,1536]{1,0:T(8,128)(2,1)S(1)}, bf16[128,1536]{1,0:T(8,128)(2,1)}, u32[]{:S(2)}) copy-start(bf16[128,1536]{1,0:T(8,128)(2,1)} %param.6) | copy-start | bytes 1179652
  54.1 78.6 %copy-start.2 = (bf16[64,768]{1,0:T(8,128)(2,1)S(1)}, bf16[64,768]{1,0:T(8,128)(2,1)}, u32[]{:S(2)}) copy-start(bf16[64,768]{1,0:T(8,128)(2,1)} %param.5) | copy-start | bytes 294916
  54.1 121.7 %all-gather.8.cloned.1.call-start = ((), (), s32[]{:S(2)}) async-start(), calls=%async_computation.7 | async-start | bytes 3538944 | tf_op jit(solution)/shard_map/all_gather | solution.py:28
  132.0 89.1 %all-gather.6.cloned.1.call-start = ((), (), s32[]{:S(2)}) async-start(), calls=%async_computation.5 | async-start | bytes 3538944 | tf_op jit(solution)/shard_map/all_gather | solution.py:45
  133.9 48.3 %all-to-all-start = ((bf16[16,64,768]{2,1,0:T(8,128)(2,1)}), bf16[16,64,768]{2,1,0:T(8,128)(2,1)}, u32[]{:S(2)}, u32[]{:S(2)}) async-start(bf16[16,64,768]{2,1,0:T(8,128)(2,1)} %stack.2), calls=%async_computation.2 | async-start | bytes 3145728 | tf_op jit(solution)/shard_map/all_to_all | solution.py:9
  139.0 217.2 %all-reduce.3.cloned.1.call-start = ((), (), s32[]{:S(2)}) async-start(), calls=%async_computation.8 | async-start | bytes 9437184 | tf_op jit(solution)/shard_map/psum | solution.py:58
  227.6 201.1 %reduce-scatter.5.cloned.1.call-start = ((), (), s32[]{:S(2)}) async-start(), calls=%async_computation.6 | async-start | bytes 3342336 | tf_op jit(solution)/shard_map/reduce_scatter | solution.py:47
Sparse Core Ops, SparseCore 0:
  9.8 38.1 all-gather.3
  54.2 75.3 reduce-scatter.2
  132.2 43.5 all-gather.7
  177.5 43.5 all-gather.5
  227.7 128.4 all-reduce.2
  358.6 70.0 reduce-scatter.4
